TPU v7x, 512 devices: a whole 4x4x16 slice. The times are simulated.
512 devices in a mesh: lat: 16 (over z), lon: 32 (over x, y, core).
Axes of the slice: x: 4, y: 4, z: 16, core: 2. Of those that a mesh axis runs over, the one named last changes fastest.
Arguments:
- diffusivity: float32 [10, 512, 4096], P(None, 'lat', 'lon'), may hold values from 0.03 to 0.24
- land_mask: int32 [512, 4096], P('lat', 'lon'), may hold values 0 or 1
- obs_weights: bfloat16 [2, 8, 512, 4096], P(None, None, 'lat', 'lon'), may hold values from -0.09375 to 0.09375
- innovation: float32 [2, 16, 32, 8], P(None, 'lat', 'lon'), may hold values from -192 to 192
- precision_weights: float32 [2, 16, 32, 8], P(None, 'lat', 'lon'), may hold values from 0.5 to 4
- obs_count: int32 [16, 32], P('lat', 'lon'), may hold values from 2 to 8, as said below
Outputs:
- control: float32 [10, 512, 4096], P(None, 'lat', 'lon')
- increment: float32 [10, 512, 4096], P(None, 'lat', 'lon')
Inputs may be any that keep to these rules, and one draw needn't show every extreme that they name: Tile (a, b) has valid observations in slots 0 to obs_count[a, b] - 1; some tile has 8.
All inputs are finite; a program needn't handle non-finite values. No bound on the sum of `land_mask` on one device may be relied on, other than what follows from the above.
Results may differ from a plain program's by a relative error of at most 0.0049.
Values sent between devices are 32-bit elements; how exact they have to be, the bound alone decides.
No kernel may reach another device: no remote copies, remote signals or barrier semaphores. Data moves between devices by JAX's collectives and lax.ppermute only.
A program may use at most 64 MiB of HBM per device.

v0:
```python
import jax
import jax.numpy as jnp
from jax import lax
from jax.sharding import PartitionSpec as P

NCAT = 5
STEPS = 6
ITERS = 2


def extended(block, sides, width):
    for axis, dim in sides:
        count = lax.axis_size(axis)
        forward = [(i, i + 1) for i in range(count - 1)]
        forward.append((count - 1, 0))
        backward = [(target, source) for source, target in forward]
        low = lax.ppermute(
            lax.slice_in_dim(block, block.shape[dim] - width, None, axis=dim), axis, forward
        )
        high = lax.ppermute(lax.slice_in_dim(block, 0, width, axis=dim), axis, backward)
        block = jnp.concatenate([low, block, high], axis=dim)
    return block


def advance(padded, east_face, north_face):
    center = padded[:, 1:-1, 1:-1]
    change = east_face[:, 1:-1, 1:] * (padded[:, 1:-1, 2:] - center)
    change = change + east_face[:, 1:-1, :-1] * (padded[:, 1:-1, :-2] - center)
    change = change + north_face[:, 1:, 1:-1] * (padded[:, 2:, 1:-1] - center)
    change = change + north_face[:, :-1, 1:-1] * (padded[:, :-2, 1:-1] - center)
    return center + change


def face_pair(grown):
    scaled = grown[:-1]
    wet = grown[-1:]
    east = 0.5 * (scaled[:, :, :-1] * wet[:, :, 1:] + scaled[:, :, 1:] * wet[:, :, :-1])
    north = 0.5 * (scaled[:, :-1, :] * wet[:, 1:, :] + scaled[:, 1:, :] * wet[:, :-1, :])
    return (east, north)


def squares(residual):
    return lax.psum(jnp.sum(residual * residual), ("lat", "lon"))


def per_device(diffusivity, land_mask, obs_weights, innovation, precision_weights, obs_count):
    ocean = land_mask.astype(jnp.float32)
    width = 1
    stacked = jnp.concatenate([diffusivity * ocean[None], ocean[None]], axis=0)
    grown = extended(stacked, (("lat", 1), ("lon", 2)), width)
    rows = grown.shape[1]
    lat_count = lax.axis_size("lat")
    lat_place = lax.axis_index("lat")
    row_ids = lax.broadcasted_iota(jnp.int32, (1, rows, 1), 1)
    outside = (lat_place == 0) & (row_ids < width) | (lat_place == lat_count - 1) & (
        row_ids >= rows - width
    )
    grown = jnp.where(outside, 0.0, grown)
    east, north = face_pair(grown)

    def extend(field):
        return extended(field, (("lat", 1), ("lon", 2)), width)

    def diffuse(field):
        for number in range(STEPS):
            field = advance(extend(field), east, north)
        return field

    def cover(field):
        return ocean[None] * diffuse(field)

    def cover_adjoint(field):
        return diffuse(ocean[None] * field)

    tile_rows, tile_cols = ocean.shape
    flat_weights = obs_weights.reshape(2, obs_weights.shape[1], tile_rows * tile_cols)
    slots = lax.broadcasted_iota(jnp.int32, innovation.shape, 3)
    keep = jnp.where(slots < obs_count[0, 0], precision_weights, 0.0)

    def spread(weighted):
        rounded = weighted.reshape(2, -1).astype(jnp.bfloat16)
        back = jnp.einsum("fok,fo->fk", flat_weights, rounded, preferred_element_type=jnp.float32)
        return jnp.repeat(back.reshape(2, tile_rows, tile_cols), NCAT, axis=0)

    right = cover_adjoint(spread(keep * innovation))
    control = jnp.zeros_like(right)
    residual = right
    direction = right
    norm_now = squares(residual)
    for number in range(ITERS):
        total = (
            cover(direction).reshape(2, NCAT, tile_rows, tile_cols).sum(axis=1).astype(jnp.bfloat16)
        )
        seen = jnp.einsum(
            "fok,fk->fo", flat_weights, total.reshape(2, -1), preferred_element_type=jnp.float32
        )
        image = direction + cover_adjoint(spread(keep * seen.reshape(innovation.shape)))
        alpha = norm_now / lax.psum(jnp.sum(direction * image), ("lat", "lon"))
        control = control + alpha * direction
        residual = residual - alpha * image
        if number + 1 < ITERS:
            norm_next = squares(residual)
            direction = residual + norm_next / norm_now * direction
            norm_now = norm_next
    return (control, cover(control))


def solution(mesh):
    return jax.shard_map(
        per_device,
        mesh=mesh,
        in_specs=(
            P(None, "lat", "lon"),
            P("lat", "lon"),
            P(None, None, "lat", "lon"),
            P(None, "lat", "lon", None),
            P(None, "lat", "lon", None),
            P("lat", "lon"),
        ),
        out_specs=(P(None, "lat", "lon"), P(None, "lat", "lon")),
        check_vma=False,
    )
```

profile of v0, /device:TPU:32, one launch (start us, length us, event | category | flops | bytes accessed | tf_op | source)
XLA Modules:
  0.0 1115.8 jit_solution(14542681047439211866)
XLA Ops:
  4.0 7.4 collective-permute-start.5
  15.3 6.0 collective-permute-start.1
  24.7 7.0 collective-permute-start.3
  37.3 7.0 collective-permute-done.7
  44.7 5.1 collective-permute-start.9
  51.8 5.1 collective-permute-done.8
  62.2 7.1 collective-permute-done.11
  69.7 5.1 collective-permute-start.13
  85.7 7.1 collective-permute-done.15
  107.2 7.1 collective-permute-done.19
  128.7 7.1 collective-permute-done.23
  151.0 7.1 collective-permute-done.27
  173.3 7.1 collective-permute-done.31
  194.8 7.1 collective-permute-done.35
  216.3 7.1 collective-permute-done.39
  238.3 7.1 collective-permute-done.43
  260.6 7.1 collective-permute-done.47
  282.1 7.1 collective-permute-done.51
  304.1 7.1 collective-permute-done.55
  325.6 7.1 collective-permute-done.59
  347.1 7.1 collective-permute-done.63
  368.6 7.1 collective-permute-done.67
  390.2 7.1 collective-permute-done.71
  411.9 7.1 collective-permute-done.75
  420.0 99.2 %all-reduce = (f32[]{:T(128)}, f32[]{:T(128)}) all-reduce(f32[]{:T(128)} %get-tuple-element.3, f32[]{:T(128)} %get-tuple-element.2), channel_id=1, replica_groups=mesh['lat'=16,'lon'=32] {'lat','lon'}, use_global_device_ids=true, to_apply=%region_1.2 | all-reduce | flops 2 | bytes 16 | tf_op jit(solution)/shard_map/psum | solution.py:43
  521.2 99.6 %psum.30 = f32[]{:T(128)} all-reduce(f32[]{:T(128)} %multiply_reduce_fusion), channel_id=1, replica_groups=mesh['lat'=16,'lon'=32] {'lat','lon'}, use_global_device_ids=true, to_apply=%region_6.7 | all-reduce | flops 1 | bytes 8 | tf_op jit(solution)/shard_map/psum | solution.py:43
  635.9 7.1 collective-permute-done.79
  643.4 4.3 collective-permute-start.81
  658.5 7.1 collective-permute-done.83
  680.3 7.1 collective-permute-done.87
  702.3 7.1 collective-permute-done.91
  723.8 7.1 collective-permute-done.95
  746.1 7.1 collective-permute-done.99
  768.2 7.1 collective-permute-done.103
  790.2 7.1 collective-permute-done.107
  811.7 7.1 collective-permute-done.111
  834.0 7.1 collective-permute-done.115
  855.5 7.1 collective-permute-done.119
  877.0 7.1 collective-permute-done.123
  885.1 98.3 %psum.31 = f32[]{:T(128)} all-reduce(f32[]{:T(128)} %fusion.4), channel_id=1, replica_groups=mesh['lat'=16,'lon'=32] {'lat','lon'}, use_global_device_ids=true, to_apply=%region_9.10 | all-reduce | flops 1 | bytes 8 | tf_op jit(solution)/shard_map/psum | solution.py:98
  986.7 3.9 collective-permute-start.124
  998.3 7.1 collective-permute-done.127
  1005.8 4.9 collective-permute-start.129
  1021.5 7.1 collective-permute-done.131
  1043.0 7.1 collective-permute-done.135
  1064.5 7.1 collective-permute-done.139
  1086.0 7.1 collective-permute-done.143
  1107.6 7.1 collective-permute-done.147
  (439 shorter events, 504.9 us)
Async XLA Ops:
  4.0 17.3 %collective-permute-start.5 = (f32[10,1,128]{2,1,0:T(1,128)S(1)}, f32[10,1,128]{2,1,0:T(1,128)S(1)}, u32[]{:S(2)}, u32[]{:S(2)}) collective-permute-start(f32[10,1,128]{2,1,0:T(1,128)S(1)} %get-tuple-element.157), channel_id=1, source_target_pairs={{32,0},{64,32},{96,64},{128,96},{160,128},{192,160},{224,192},{256... | collective-permute-start | bytes 15368 | tf_op jit(solution)/shard_map/ppermute | solution.py:20
  11.4 9.9 collective-permute-start.4
  13.3 8.0 collective-permute-start
  15.3 7.4 collective-permute-start.1
  22.8 13.4 %collective-permute-start.2 = (f32[11,34,1]{2,1,0:T(8,128)S(1)}, f32[11,34,1]{2,1,0:T(8,128)S(1)}, u32[]{:S(2)}, u32[]{:S(2)}) collective-permute-start(f32[11,34,1]{2,1,0:T(8,128)S(1)} %get-tuple-element.11), channel_id=1, source_target_pairs={{0,1},{1,2},{2,3},{3,4},{4,5},{5,6},{6,7},{7,8},{8,9},{9,10},{10,1... | collective-permute-start | bytes 4496 | tf_op jit(solution)/shard_map/ppermute | solution.py:17
  24.7 11.4 %collective-permute-start.3 = (f32[11,34,1]{2,1,0:T(8,128)S(1)}, f32[11,34,1]{2,1,0:T(8,128)S(1)}, u32[]{:S(2)}, u32[]{:S(2)}) collective-permute-start(f32[11,34,1]{2,1,0:T(8,128)S(1)} %get-tuple-element.12), channel_id=1, source_target_pairs={{1,0},{2,1},{3,2},{4,3},{5,4},{6,5},{7,6},{8,7},{9,8},{10,9},{11,1... | collective-permute-start | bytes 4496 | tf_op jit(solution)/shard_map/ppermute | solution.py:20
  34.0 10.4 collective-permute-start.7
  44.7 7.1 collective-permute-start.9
  49.9 7.0 collective-permute-start.8
  59.0 10.4 collective-permute-start.11
  69.7 7.1 collective-permute-start.13
  82.5 10.4 collective-permute-start.15
  93.2 5.9 collective-permute-start.17
  104.0 10.4 collective-permute-start.19
  125.4 10.4 collective-permute-start.23
  147.7 10.4 collective-permute-start.27
  170.0 10.4 collective-permute-start.31
  191.5 10.4 collective-permute-start.35
  213.0 10.4 collective-permute-start.39
  235.1 10.4 collective-permute-start.43
  257.4 10.4 collective-permute-start.47
  278.9 10.4 collective-permute-start.51
  300.9 10.4 collective-permute-start.55
  322.4 10.4 collective-permute-start.59
  343.9 10.4 collective-permute-start.63
  365.4 10.4 collective-permute-start.67
  386.9 10.4 collective-permute-start.71
  408.6 10.4 collective-permute-start.75
  632.6 10.4 collective-permute-start.79
  643.4 6.2 collective-permute-start.81
  655.3 10.4 collective-permute-start.83
  677.0 10.4 collective-permute-start.87
  699.1 10.4 collective-permute-start.91
  720.6 10.4 collective-permute-start.95
  742.9 10.4 collective-permute-start.99
  764.9 10.4 collective-permute-start.103
  786.9 10.4 collective-permute-start.107
  808.4 10.4 collective-permute-start.111
  830.7 10.4 collective-permute-start.115
  852.2 10.4 collective-permute-start.119
  873.7 10.4 collective-permute-start.123
  995.0 10.4 collective-permute-start.127
  1005.8 6.8 collective-permute-start.129
  1018.2 10.4 collective-permute-start.131
  1039.7 10.4 collective-permute-start.135
  1061.3 10.4 collective-permute-start.139
  1082.7 10.4 collective-permute-start.143
  1104.4 10.4 collective-permute-start.147
  (104 other events, 574.6 us)
where the time goes:
time: 1120 us
  waiting for transfers between devices  395 us (35%)
  starting transfers between devices  391 us (35%)
  blocking collectives  297 us (27%)
  other arithmetic  17.6 us (2%)
    ppermute x74, waiting for transfers between devices, extended(): lax.ppermute(lax.slice_in_dim(block, block.shape[dim] - width, None, axis...  364 us
    ppermute x74, starting transfers between devices, extended(): lax.ppermute(lax.slice_in_dim(block, 0, width, axis=dim), axis, backward)  212 us
    psum x2, blocking collectives, squares(): return lax.psum(jnp.sum(residual * residual), ('lat', 'lon'))  199 us
    ppermute x74, starting transfers between devices, extended(): lax.ppermute(lax.slice_in_dim(block, block.shape[dim] - width, None, axis...  179 us
    psum x1, blocking collectives, per_device(): alpha = norm_now / lax.psum(jnp.sum(direction * image), ('lat', 'lon'))  98.3 us
    ppermute x74, waiting for transfers between devices, extended(): lax.ppermute(lax.slice_in_dim(block, 0, width, axis=dim), axis, backward)  31.5 us
  transfers between devices with their start and end apart: 148, of which 108 were waited for; matrix products, arithmetic and copies ran while one was open for 0% of the time, Pallas kernels for 0%

commit v1 on v0

--- a/solution.py
+++ b/solution.py
@@ -20,6 +20,15 @@
         high = lax.ppermute(lax.slice_in_dim(block, 0, width, axis=dim), axis, backward)
         block = jnp.concatenate([low, block, high], axis=dim)
     return block
+
+
+def outside_rows(rows, width):
+    lat_count = lax.axis_size("lat")
+    lat_place = lax.axis_index("lat")
+    row_ids = lax.broadcasted_iota(jnp.int32, (1, rows, 1), 1)
+    return (lat_place == 0) & (row_ids < width) | (lat_place == lat_count - 1) & (
+        row_ids >= rows - width
+    )
 
 
 def advance(padded, east_face, north_face):
@@ -45,25 +54,26 @@
 
 def per_device(diffusivity, land_mask, obs_weights, innovation, precision_weights, obs_count):
     ocean = land_mask.astype(jnp.float32)
-    width = 1
+    tile_rows, tile_cols = ocean.shape
+    width = STEPS
     stacked = jnp.concatenate([diffusivity * ocean[None], ocean[None]], axis=0)
     grown = extended(stacked, (("lat", 1), ("lon", 2)), width)
-    rows = grown.shape[1]
-    lat_count = lax.axis_size("lat")
-    lat_place = lax.axis_index("lat")
-    row_ids = lax.broadcasted_iota(jnp.int32, (1, rows, 1), 1)
-    outside = (lat_place == 0) & (row_ids < width) | (lat_place == lat_count - 1) & (
-        row_ids >= rows - width
-    )
-    grown = jnp.where(outside, 0.0, grown)
+    grown = jnp.where(outside_rows(grown.shape[1], width), 0.0, grown)
     east, north = face_pair(grown)
+    edge = outside_rows(tile_rows + 2 * width, width)
 
     def extend(field):
-        return extended(field, (("lat", 1), ("lon", 2)), width)
+        field = extended(field, (("lat", 1), ("lon", 2)), width)
+        return jnp.where(edge, 0.0, field)
 
     def diffuse(field):
+        field = extend(field)
         for number in range(STEPS):
-            field = advance(extend(field), east, north)
+            halo = width - number
+            lo = width - halo
+            east_part = east[:, lo : lo + tile_rows + 2 * halo, lo : lo + tile_cols + 2 * halo - 1]
+            north_part = north[:, lo : lo + tile_rows + 2 * halo - 1, lo : lo + tile_cols + 2 * halo]
+            field = advance(field, east_part, north_part)
         return field
 
     def cover(field):
@@ -72,7 +82,6 @@
     def cover_adjoint(field):
         return diffuse(ocean[None] * field)
 
-    tile_rows, tile_cols = ocean.shape
     flat_weights = obs_weights.reshape(2, obs_weights.shape[1], tile_rows * tile_cols)
     slots = lax.broadcasted_iota(jnp.int32, innovation.shape, 3)
     keep = jnp.where(slots < obs_count[0, 0], precision_weights, 0.0)

time: 1120 us -> 515 us (0.46)
  the two profiles are of different devices: /device:TPU:32 before, /device:TPU:31 now
where the time goes in v1:
time: 515 us; the launch traced here: 507 us
  blocking collectives  301 us (58%)
  starting transfers between devices  101 us (20%)
  waiting for transfers between devices  58.6 us (11%)
  other arithmetic  36.8 us (7%)
  between operations  6.52 us (1%)
    psum x2, blocking collectives, squares(): return lax.psum(jnp.sum(residual * residual), ('lat', 'lon'))  200 us
    psum x1, blocking collectives, per_device(): alpha = norm_now / lax.psum(jnp.sum(direction * image), ('lat', 'lon'))  100 us
    ppermute x14, waiting for transfers between devices, extended(): lax.ppermute(lax.slice_in_dim(block, 0, width, axis=dim), axis, backward)  52.5 us
    ppermute x14, starting transfers between devices, extended(): lax.ppermute(lax.slice_in_dim(block, 0, width, axis=dim), axis, backward)  50.5 us
    ppermute x14, starting transfers between devices, extended(): lax.ppermute(lax.slice_in_dim(block, block.shape[dim] - width, None, axis...  50.3 us
    add x31, other arithmetic, advance(): return center + change  28.6 us
  transfers between devices with their start and end apart: 28, of which 17 were waited for; matrix products, arithmetic and copies ran while one was open for 0% of the time, Pallas kernels for 0%

profile of v1, /device:TPU:31, one launch (start us, length us, event | category | flops | bytes accessed | tf_op | source)
XLA Modules:
  0.0 507.3 jit_solution(12809474704723728463)
XLA Ops:
  4.0 3.5 collective-permute-start
  7.5 9.5 %collective-permute-start.1 = (f32[10,6,128]{2,1,0:T(8,128)S(1)}, f32[10,6,128]{2,1,0:T(8,128)S(1)}, u32[]{:S(2)}, u32[]{:S(2)}) collective-permute-start(f32[10,6,128]{2,1,0:T(8,128)S(1)} %get-tuple-element.38), channel_id=1, source_target_pairs={{32,0},{64,32},{96,64},{128,96},{160,128},{192,160},{224,192},{256... | collective-permute-start | bytes 92168 | tf_op jit(solution)/shard_map/ppermute | solution.py:20
  17.1 1.9 collective-permute-start.4
  19.0 4.6 collective-permute-start.5
  23.8 3.2 collective-permute-start.2
  26.9 2.2 collective-permute-start.3
  29.3 6.7 %collective-permute-start.6 = (f32[11,44,6]{2,1,0:T(8,128)S(1)}, f32[11,44,6]{2,1,0:T(8,128)S(1)}, u32[]{:S(2)}, u32[]{:S(2)}) collective-permute-start(f32[11,44,6]{2,1,0:T(8,128)S(1)} %get-tuple-element.11), channel_id=1, source_target_pairs={{0,1},{1,2},{2,3},{3,4},{4,5},{5,6},{6,7},{7,8},{8,9},{9,10},{10,1... | collective-permute-start | bytes 34856 | tf_op jit(solution)/shard_map/ppermute | solution.py:17
  36.0 1.9 collective-permute-start.7
  38.3 1.1 collective-permute-done.6
  39.4 7.7 %collective-permute-done.7 = f32[11,44,6]{2,1,0:T(8,128)S(1)} collective-permute-done((f32[11,44,6]{2,1,0:T(8,128)S(1)}, f32[11,44,6]{2,1,0:T(8,128)S(1)}, u32[]{:S(2)}, u32[]{:S(2)}) %collective-permute-start.7) | collective-permute-done | bytes 11648 | tf_op jit(solution)/shard_map/ppermute | solution.py:20
  53.1 1.9 collective-permute-start.8
  55.0 4.6 collective-permute-start.9
  59.6 1.1 collective-permute-done.9
  60.8 2.9 collective-permute-start.10
  63.7 2.4 collective-permute-start.11
  66.8 7.7 %collective-permute-done.11 = f32[10,44,6]{2,1,0:T(8,128)S(1)} collective-permute-done((f32[10,44,6]{2,1,0:T(8,128)S(1)}, f32[10,44,6]{2,1,0:T(8,128)S(1)}, u32[]{:S(2)}, u32[]{:S(2)}) %collective-permute-start.11) | collective-permute-done | bytes 10592 | tf_op jit(solution)/shard_map/ppermute | solution.py:20
  80.5 1.9 collective-permute-start.12
  82.5 5.2 %collective-permute-start.13 = (f32[10,6,128]{2,1,0:T(8,128)S(1)}, f32[10,6,128]{2,1,0:T(8,128)S(1)}, u32[]{:S(2)}, u32[]{:S(2)}) collective-permute-start(f32[10,6,128]{2,1,0:T(8,128)S(1)} %get-tuple-element.34), channel_id=1, source_target_pairs={{32,0},{64,32},{96,64},{128,96},{160,128},{192,160},{224,192},{256... | collective-permute-start | bytes 92168 | tf_op jit(solution)/shard_map/ppermute | solution.py:20
  87.6 1.1 collective-permute-done.13
  88.9 2.6 collective-permute-start.14
  91.5 1.9 collective-permute-start.15
  93.4 1.2 collective-permute-done.14
  94.6 7.7 %collective-permute-done.15 = f32[10,44,6]{2,1,0:T(8,128)S(1)} collective-permute-done((f32[10,44,6]{2,1,0:T(8,128)S(1)}, f32[10,44,6]{2,1,0:T(8,128)S(1)}, u32[]{:S(2)}, u32[]{:S(2)}) %collective-permute-start.15) | collective-permute-done | bytes 10592 | tf_op jit(solution)/shard_map/ppermute | solution.py:20
  107.4 1.0 multiply_reduce_fusion.1
  108.4 101.8 %all-reduce = (f32[]{:T(128)}, f32[]{:T(128)}) all-reduce(f32[]{:T(128)} %get-tuple-element.3, f32[]{:T(128)} %get-tuple-element.2), channel_id=1, replica_groups=mesh['lat'=16,'lon'=32] {'lat','lon'}, use_global_device_ids=true, to_apply=%region_1.2 | all-reduce | flops 2 | bytes 16 | tf_op jit(solution)/shard_map/psum | solution.py:52
  212.1 98.7 %psum.30 = f32[]{:T(128)} all-reduce(f32[]{:T(128)} %multiply_reduce_fusion), channel_id=1, replica_groups=mesh['lat'=16,'lon'=32] {'lat','lon'}, use_global_device_ids=true, to_apply=%region_6.7 | all-reduce | flops 1 | bytes 8 | tf_op jit(solution)/shard_map/psum | solution.py:52
  312.3 3.7 collective-permute-start.16
  315.9 2.8 collective-permute-start.17
  318.8 1.9 collective-permute-done.17
  320.9 7.5 %collective-permute-start.18 = (f32[10,44,6]{2,1,0:T(8,128)S(1)}, f32[10,44,6]{2,1,0:T(8,128)S(1)}, u32[]{:S(2)}, u32[]{:S(2)}) collective-permute-start(f32[10,44,6]{2,1,0:T(8,128)S(1)} %get-tuple-element.17), channel_id=1, source_target_pairs={{0,1},{1,2},{2,3},{3,4},{4,5},{5,6},{6,7},{7,8},{8,9},{9,10},{10,1... | collective-permute-start | bytes 31688 | tf_op jit(solution)/shard_map/ppermute | solution.py:17
  328.4 1.9 collective-permute-start.19
  330.3 1.2 collective-permute-done.18
  331.5 7.7 %collective-permute-done.19 = f32[10,44,6]{2,1,0:T(8,128)S(1)} collective-permute-done((f32[10,44,6]{2,1,0:T(8,128)S(1)}, f32[10,44,6]{2,1,0:T(8,128)S(1)}, u32[]{:S(2)}, u32[]{:S(2)}) %collective-permute-start.19) | collective-permute-done | bytes 10592 | tf_op jit(solution)/shard_map/ppermute | solution.py:20
  345.2 1.9 collective-permute-start.20
  347.1 4.6 collective-permute-start.21
  351.7 1.1 collective-permute-done.21
  352.9 2.9 collective-permute-start.22
  355.8 2.1 collective-permute-start.23
  358.9 7.7 %collective-permute-done.23 = f32[10,44,6]{2,1,0:T(8,128)S(1)} collective-permute-done((f32[10,44,6]{2,1,0:T(8,128)S(1)}, f32[10,44,6]{2,1,0:T(8,128)S(1)}, u32[]{:S(2)}, u32[]{:S(2)}) %collective-permute-start.23) | collective-permute-done | bytes 10592 | tf_op jit(solution)/shard_map/ppermute | solution.py:20
  371.7 1.0 fusion.244
  372.7 100.4 %psum.31 = f32[]{:T(128)} all-reduce(f32[]{:T(128)} %fusion.244), channel_id=1, replica_groups=mesh['lat'=16,'lon'=32] {'lat','lon'}, use_global_device_ids=true, to_apply=%region_9.10 | all-reduce | flops 1 | bytes 8 | tf_op jit(solution)/shard_map/psum | solution.py:107
  474.6 1.9 collective-permute-start.24
  476.5 4.6 collective-permute-start.25
  481.1 1.1 collective-permute-done.25
  482.3 7.7 %collective-permute-start.26 = (f32[10,44,6]{2,1,0:T(8,128)S(1)}, f32[10,44,6]{2,1,0:T(8,128)S(1)}, u32[]{:S(2)}, u32[]{:S(2)}) collective-permute-start(f32[10,44,6]{2,1,0:T(8,128)S(1)} %get-tuple-element.13), channel_id=1, source_target_pairs={{0,1},{1,2},{2,3},{3,4},{4,5},{5,6},{6,7},{7,8},{8,9},{9,10},{10,1... | collective-permute-start | bytes 31688 | tf_op jit(solution)/shard_map/ppermute | solution.py:17
  490.0 2.2 collective-permute-start.27
  493.2 7.7 %collective-permute-done.27 = f32[10,44,6]{2,1,0:T(8,128)S(1)} collective-permute-done((f32[10,44,6]{2,1,0:T(8,128)S(1)}, f32[10,44,6]{2,1,0:T(8,128)S(1)}, u32[]{:S(2)}, u32[]{:S(2)}) %collective-permute-start.27) | collective-permute-done | bytes 10592 | tf_op jit(solution)/shard_map/ppermute | solution.py:20
  505.9 1.1 fusion.248
  (115 shorter events, 39.9 us)
Async XLA Ops:
  2.0 1.0 copy-start.2
  2.0 1.0 copy-start.3
  3.0 0.9 copy-start.1
  4.0 19.6 %collective-permute-start = (f32[10,6,128]{2,1,0:T(8,128)S(1)}, f32[10,6,128]{2,1,0:T(8,128)S(1)}, u32[]{:S(2)}, u32[]{:S(2)}) collective-permute-start(f32[10,6,128]{2,1,0:T(8,128)S(1)} %get-tuple-element.37), channel_id=1, source_target_pairs={{0,32},{32,64},{64,96},{96,128},{128,160},{160,192},{192,224},{224... | collective-permute-start | bytes 92168 | tf_op jit(solution)/shard_map/ppermute | solution.py:17
  7.5 16.1 %collective-permute-start.1 = (f32[10,6,128]{2,1,0:T(8,128)S(1)}, f32[10,6,128]{2,1,0:T(8,128)S(1)}, u32[]{:S(2)}, u32[]{:S(2)}) collective-permute-start(f32[10,6,128]{2,1,0:T(8,128)S(1)} %get-tuple-element.38), channel_id=1, source_target_pairs={{32,0},{64,32},{96,64},{128,96},{160,128},{192,160},{224,192},{256... | collective-permute-start | bytes 92168 | tf_op jit(solution)/shard_map/ppermute | solution.py:20
  17.1 12.1 %collective-permute-start.4 = (f32[11,6,128]{2,1,0:T(8,128)S(1)}, f32[11,6,128]{2,1,0:T(8,128)S(1)}, u32[]{:S(2)}, u32[]{:S(2)}) collective-permute-start(f32[11,6,128]{2,1,0:T(8,128)S(1)} %get-tuple-element.25), channel_id=1, source_target_pairs={{0,32},{32,64},{64,96},{96,128},{128,160},{160,192},{192,224},{224... | collective-permute-start | bytes 101384 | tf_op jit(solution)/shard_map/ppermute | solution.py:17
  19.0 10.2 %collective-permute-start.5 = (f32[11,6,128]{2,1,0:T(8,128)S(1)}, f32[11,6,128]{2,1,0:T(8,128)S(1)}, u32[]{:S(2)}, u32[]{:S(2)}) collective-permute-start(f32[11,6,128]{2,1,0:T(8,128)S(1)} %get-tuple-element.26), channel_id=1, source_target_pairs={{32,0},{64,32},{96,64},{128,96},{160,128},{192,160},{224,192},{256... | collective-permute-start | bytes 101384 | tf_op jit(solution)/shard_map/ppermute | solution.py:20
  23.8 14.2 %collective-permute-start.2 = (f32[10,44,6]{2,1,0:T(8,128)S(1)}, f32[10,44,6]{2,1,0:T(8,128)S(1)}, u32[]{:S(2)}, u32[]{:S(2)}) collective-permute-start(f32[10,44,6]{2,1,0:T(8,128)S(1)} %get-tuple-element.23), channel_id=1, source_target_pairs={{0,1},{1,2},{2,3},{3,4},{4,5},{5,6},{6,7},{7,8},{8,9},{9,10},{10,1... | collective-permute-start | bytes 31688 | tf_op jit(solution)/shard_map/ppermute | solution.py:17
  26.9 11.0 %collective-permute-start.3 = (f32[10,44,6]{2,1,0:T(8,128)S(1)}, f32[10,44,6]{2,1,0:T(8,128)S(1)}, u32[]{:S(2)}, u32[]{:S(2)}) collective-permute-start(f32[10,44,6]{2,1,0:T(8,128)S(1)} %get-tuple-element.24), channel_id=1, source_target_pairs={{1,0},{2,1},{3,2},{4,3},{5,4},{6,5},{7,6},{8,7},{9,8},{10,9},{11,1... | collective-permute-start | bytes 31688 | tf_op jit(solution)/shard_map/ppermute | solution.py:20
  29.3 10.1 %collective-permute-start.6 = (f32[11,44,6]{2,1,0:T(8,128)S(1)}, f32[11,44,6]{2,1,0:T(8,128)S(1)}, u32[]{:S(2)}, u32[]{:S(2)}) collective-permute-start(f32[11,44,6]{2,1,0:T(8,128)S(1)} %get-tuple-element.11), channel_id=1, source_target_pairs={{0,1},{1,2},{2,3},{3,4},{4,5},{5,6},{6,7},{7,8},{8,9},{9,10},{10,1... | collective-permute-start | bytes 34856 | tf_op jit(solution)/shard_map/ppermute | solution.py:17
  36.0 11.1 %collective-permute-start.7 = (f32[11,44,6]{2,1,0:T(8,128)S(1)}, f32[11,44,6]{2,1,0:T(8,128)S(1)}, u32[]{:S(2)}, u32[]{:S(2)}) collective-permute-start(f32[11,44,6]{2,1,0:T(8,128)S(1)} %get-tuple-element.12), channel_id=1, source_target_pairs={{1,0},{2,1},{3,2},{4,3},{5,4},{6,5},{7,6},{8,7},{9,8},{10,9},{11,1... | collective-permute-start | bytes 34856 | tf_op jit(solution)/shard_map/ppermute | solution.py:20
  53.1 6.5 %collective-permute-start.8 = (f32[10,6,128]{2,1,0:T(8,128)S(1)}, f32[10,6,128]{2,1,0:T(8,128)S(1)}, u32[]{:S(2)}, u32[]{:S(2)}) collective-permute-start(f32[10,6,128]{2,1,0:T(8,128)S(1)} %get-tuple-element.35), channel_id=1, source_target_pairs={{0,32},{32,64},{64,96},{96,128},{128,160},{160,192},{192,224},{224... | collective-permute-start | bytes 92168 | tf_op jit(solution)/shard_map/ppermute | solution.py:17
  55.0 5.7 %collective-permute-start.9 = (f32[10,6,128]{2,1,0:T(8,128)S(1)}, f32[10,6,128]{2,1,0:T(8,128)S(1)}, u32[]{:S(2)}, u32[]{:S(2)}) collective-permute-start(f32[10,6,128]{2,1,0:T(8,128)S(1)} %get-tuple-element.36), channel_id=1, source_target_pairs={{32,0},{64,32},{96,64},{128,96},{160,128},{192,160},{224,192},{256... | collective-permute-start | bytes 92168 | tf_op jit(solution)/shard_map/ppermute | solution.py:20
  60.8 6.0 %collective-permute-start.10 = (f32[10,44,6]{2,1,0:T(8,128)S(1)}, f32[10,44,6]{2,1,0:T(8,128)S(1)}, u32[]{:S(2)}, u32[]{:S(2)}) collective-permute-start(f32[10,44,6]{2,1,0:T(8,128)S(1)} %get-tuple-element.21), channel_id=1, source_target_pairs={{0,1},{1,2},{2,3},{3,4},{4,5},{5,6},{6,7},{7,8},{8,9},{9,10},{10,1... | collective-permute-start | bytes 31688 | tf_op jit(solution)/shard_map/ppermute | solution.py:17
  63.7 10.8 %collective-permute-start.11 = (f32[10,44,6]{2,1,0:T(8,128)S(1)}, f32[10,44,6]{2,1,0:T(8,128)S(1)}, u32[]{:S(2)}, u32[]{:S(2)}) collective-permute-start(f32[10,44,6]{2,1,0:T(8,128)S(1)} %get-tuple-element.22), channel_id=1, source_target_pairs={{1,0},{2,1},{3,2},{4,3},{5,4},{6,5},{7,6},{8,7},{9,8},{10,9},{11,1... | collective-permute-start | bytes 31688 | tf_op jit(solution)/shard_map/ppermute | solution.py:20
  80.5 7.1 %collective-permute-start.12 = (f32[10,6,128]{2,1,0:T(8,128)S(1)}, f32[10,6,128]{2,1,0:T(8,128)S(1)}, u32[]{:S(2)}, u32[]{:S(2)}) collective-permute-start(f32[10,6,128]{2,1,0:T(8,128)S(1)} %get-tuple-element.33), channel_id=1, source_target_pairs={{0,32},{32,64},{64,96},{96,128},{128,160},{160,192},{192,224},{224... | collective-permute-start | bytes 92168 | tf_op jit(solution)/shard_map/ppermute | solution.py:17
  82.5 6.3 %collective-permute-start.13 = (f32[10,6,128]{2,1,0:T(8,128)S(1)}, f32[10,6,128]{2,1,0:T(8,128)S(1)}, u32[]{:S(2)}, u32[]{:S(2)}) collective-permute-start(f32[10,6,128]{2,1,0:T(8,128)S(1)} %get-tuple-element.34), channel_id=1, source_target_pairs={{32,0},{64,32},{96,64},{128,96},{160,128},{192,160},{224,192},{256... | collective-permute-start | bytes 92168 | tf_op jit(solution)/shard_map/ppermute | solution.py:20
  88.9 5.7 %collective-permute-start.14 = (f32[10,44,6]{2,1,0:T(8,128)S(1)}, f32[10,44,6]{2,1,0:T(8,128)S(1)}, u32[]{:S(2)}, u32[]{:S(2)}) collective-permute-start(f32[10,44,6]{2,1,0:T(8,128)S(1)} %get-tuple-element.19), channel_id=1, source_target_pairs={{0,1},{1,2},{2,3},{3,4},{4,5},{5,6},{6,7},{7,8},{8,9},{9,10},{10,1... | collective-permute-start | bytes 31688 | tf_op jit(solution)/shard_map/ppermute | solution.py:17
  91.5 10.8 %collective-permute-start.15 = (f32[10,44,6]{2,1,0:T(8,128)S(1)}, f32[10,44,6]{2,1,0:T(8,128)S(1)}, u32[]{:S(2)}, u32[]{:S(2)}) collective-permute-start(f32[10,44,6]{2,1,0:T(8,128)S(1)} %get-tuple-element.20), channel_id=1, source_target_pairs={{1,0},{2,1},{3,2},{4,3},{5,4},{6,5},{7,6},{8,7},{9,8},{10,9},{11,1... | collective-permute-start | bytes 31688 | tf_op jit(solution)/shard_map/ppermute | solution.py:20
  312.3 6.5 %collective-permute-start.16 = (f32[10,6,128]{2,1,0:T(8,128)S(1)}, f32[10,6,128]{2,1,0:T(8,128)S(1)}, u32[]{:S(2)}, u32[]{:S(2)}) collective-permute-start(f32[10,6,128]{2,1,0:T(8,128)S(1)} %get-tuple-element.31), channel_id=1, source_target_pairs={{0,32},{32,64},{64,96},{96,128},{128,160},{160,192},{192,224},{224... | collective-permute-start | bytes 92168 | tf_op jit(solution)/shard_map/ppermute | solution.py:17
  315.9 4.7 collective-permute-start.17
  320.9 10.6 %collective-permute-start.18 = (f32[10,44,6]{2,1,0:T(8,128)S(1)}, f32[10,44,6]{2,1,0:T(8,128)S(1)}, u32[]{:S(2)}, u32[]{:S(2)}) collective-permute-start(f32[10,44,6]{2,1,0:T(8,128)S(1)} %get-tuple-element.17), channel_id=1, source_target_pairs={{0,1},{1,2},{2,3},{3,4},{4,5},{5,6},{6,7},{7,8},{8,9},{9,10},{10,1... | collective-permute-start | bytes 31688 | tf_op jit(solution)/shard_map/ppermute | solution.py:17
  328.4 10.8 %collective-permute-start.19 = (f32[10,44,6]{2,1,0:T(8,128)S(1)}, f32[10,44,6]{2,1,0:T(8,128)S(1)}, u32[]{:S(2)}, u32[]{:S(2)}) collective-permute-start(f32[10,44,6]{2,1,0:T(8,128)S(1)} %get-tuple-element.18), channel_id=1, source_target_pairs={{1,0},{2,1},{3,2},{4,3},{5,4},{6,5},{7,6},{8,7},{9,8},{10,9},{11,1... | collective-permute-start | bytes 31688 | tf_op jit(solution)/shard_map/ppermute | solution.py:20
  345.2 6.5 %collective-permute-start.20 = (f32[10,6,128]{2,1,0:T(8,128)S(1)}, f32[10,6,128]{2,1,0:T(8,128)S(1)}, u32[]{:S(2)}, u32[]{:S(2)}) collective-permute-start(f32[10,6,128]{2,1,0:T(8,128)S(1)} %get-tuple-element.29), channel_id=1, source_target_pairs={{0,32},{32,64},{64,96},{96,128},{128,160},{160,192},{192,224},{224... | collective-permute-start | bytes 92168 | tf_op jit(solution)/shard_map/ppermute | solution.py:17
  347.1 5.7 %collective-permute-start.21 = (f32[10,6,128]{2,1,0:T(8,128)S(1)}, f32[10,6,128]{2,1,0:T(8,128)S(1)}, u32[]{:S(2)}, u32[]{:S(2)}) collective-permute-start(f32[10,6,128]{2,1,0:T(8,128)S(1)} %get-tuple-element.30), channel_id=1, source_target_pairs={{32,0},{64,32},{96,64},{128,96},{160,128},{192,160},{224,192},{256... | collective-permute-start | bytes 92168 | tf_op jit(solution)/shard_map/ppermute | solution.py:20
  352.9 6.0 %collective-permute-start.22 = (f32[10,44,6]{2,1,0:T(8,128)S(1)}, f32[10,44,6]{2,1,0:T(8,128)S(1)}, u32[]{:S(2)}, u32[]{:S(2)}) collective-permute-start(f32[10,44,6]{2,1,0:T(8,128)S(1)} %get-tuple-element.15), channel_id=1, source_target_pairs={{0,1},{1,2},{2,3},{3,4},{4,5},{5,6},{6,7},{7,8},{8,9},{9,10},{10,1... | collective-permute-start | bytes 31688 | tf_op jit(solution)/shard_map/ppermute | solution.py:17
  355.8 10.8 %collective-permute-start.23 = (f32[10,44,6]{2,1,0:T(8,128)S(1)}, f32[10,44,6]{2,1,0:T(8,128)S(1)}, u32[]{:S(2)}, u32[]{:S(2)}) collective-permute-start(f32[10,44,6]{2,1,0:T(8,128)S(1)} %get-tuple-element.16), channel_id=1, source_target_pairs={{1,0},{2,1},{3,2},{4,3},{5,4},{6,5},{7,6},{8,7},{9,8},{10,9},{11,1... | collective-permute-start | bytes 31688 | tf_op jit(solution)/shard_map/ppermute | solution.py:20
  474.5 26.3 %copy-start = (f32[10,32,128]{2,1,0:T(8,128)}, f32[10,32,128]{2,1,0:T(8,128)S(1)}, u32[]{:S(2)}) copy-start(f32[10,32,128]{2,1,0:T(8,128)S(1)} %multiply_add_fusion) | copy-start | bytes 491524
  474.6 6.5 %collective-permute-start.24 = (f32[10,6,128]{2,1,0:T(8,128)S(1)}, f32[10,6,128]{2,1,0:T(8,128)S(1)}, u32[]{:S(2)}, u32[]{:S(2)}) collective-permute-start(f32[10,6,128]{2,1,0:T(8,128)S(1)} %get-tuple-element.27), channel_id=1, source_target_pairs={{0,32},{32,64},{64,96},{96,128},{128,160},{160,192},{192,224},{224... | collective-permute-start | bytes 92168 | tf_op jit(solution)/shard_map/ppermute | solution.py:17
  476.5 5.7 %collective-permute-start.25 = (f32[10,6,128]{2,1,0:T(8,128)S(1)}, f32[10,6,128]{2,1,0:T(8,128)S(1)}, u32[]{:S(2)}, u32[]{:S(2)}) collective-permute-start(f32[10,6,128]{2,1,0:T(8,128)S(1)} %get-tuple-element.28), channel_id=1, source_target_pairs={{32,0},{64,32},{96,64},{128,96},{160,128},{192,160},{224,192},{256... | collective-permute-start | bytes 92168 | tf_op jit(solution)/shard_map/ppermute | solution.py:20
  482.3 10.8 %collective-permute-start.26 = (f32[10,44,6]{2,1,0:T(8,128)S(1)}, f32[10,44,6]{2,1,0:T(8,128)S(1)}, u32[]{:S(2)}, u32[]{:S(2)}) collective-permute-start(f32[10,44,6]{2,1,0:T(8,128)S(1)} %get-tuple-element.13), channel_id=1, source_target_pairs={{0,1},{1,2},{2,3},{3,4},{4,5},{5,6},{6,7},{7,8},{8,9},{9,10},{10,1... | collective-permute-start | bytes 31688 | tf_op jit(solution)/shard_map/ppermute | solution.py:17
  490.0 10.8 %collective-permute-start.27 = (f32[10,44,6]{2,1,0:T(8,128)S(1)}, f32[10,44,6]{2,1,0:T(8,128)S(1)}, u32[]{:S(2)}, u32[]{:S(2)}) collective-permute-start(f32[10,44,6]{2,1,0:T(8,128)S(1)} %get-tuple-element.14), channel_id=1, source_target_pairs={{1,0},{2,1},{3,2},{4,3},{5,4},{6,5},{7,6},{8,7},{9,8},{10,9},{11,1... | collective-permute-start | bytes 31688 | tf_op jit(solution)/shard_map/ppermute | solution.py:20
